TPU v7x, 256 devices: a whole 4x4x8 slice. The times are simulated.
256 devices in a mesh: dp: 8 (over z), ctx: 32 (over y, x, core).
Axes of the slice: x: 4, y: 4, z: 8, core: 2. Of those that a mesh axis runs over, the one named last changes fastest.
Arguments:
- queries: bfloat16 [8, 4096, 2048], P('dp', 'ctx'), may hold values from -6 to 6
- keys: bfloat16 [8, 4096, 2048], P('dp', 'ctx'), may hold values from -6 to 6
- values: bfloat16 [8, 4096, 2048], P('dp', 'ctx'), may hold values from -6 to 6
- grad_output: bfloat16 [8, 4096, 2048], P('dp', 'ctx'), may hold values from -6 to 6
- out_gain: float32 [2048], replicated, may hold values from 0.5 to 1.5
- doc_lengths: int32 [8, 12], P('dp'), may hold values from 1 to 1365, 4096 in all within a row
Outputs:
- output: bfloat16 [8, 4096, 2048], P('dp', 'ctx')
- grad_queries: bfloat16 [8, 4096, 2048], P('dp', 'ctx')
- grad_keys: bfloat16 [8, 4096, 2048], P('dp', 'ctx')
- grad_values: bfloat16 [8, 4096, 2048], P('dp', 'ctx')
- grad_gain: float32 [2048], replicated
Inputs may be any that keep to these rules, and one draw needn't show every extreme that they name: `doc_lengths`: each row holds the lengths of 12 documents packed end to end; they sum to 4096, and the largest is exactly 1365.
All inputs are finite; a program needn't handle non-finite values.
Results may differ from a plain program's by a relative error of at most 0.012.
The roundings to bfloat16 on the way count: a program that leaves them out, or rounds other values in their place, can miss the bound.
Values may be sent and summed in bfloat16 or wider, within the bound.
No kernel may reach another device: no remote copies, remote signals or barrier semaphores. Data moves between devices by JAX's collectives and lax.ppermute only.
A program may use at most 64 MiB of HBM per device.

v0:
```python
import math
import jax
import jax.numpy as jnp
from jax import lax
from jax.sharding import PartitionSpec as P

H = 32
E = 64
eps = 1e-05


def entering(part, axis, combine, identity):
    place = lax.axis_index(axis)
    gathered = jax.tree.map(lambda a: lax.all_gather(a, axis), part)
    state = jax.tree.map(lambda a, e: jnp.zeros_like(a) + jnp.asarray(e, a.dtype), part, identity)

    def entering_one(step, state):
        return combine(
            state, jax.tree.map(lambda a: lax.dynamic_index_in_dim(a, step, 0, False), gathered)
        )

    return lax.fori_loop(0, place, entering_one, state)


def carried_in(shard, axis, join, neutral):
    count = lax.axis_size(axis)
    place = lax.axis_index(axis)
    ahead = count - 1 - place
    gathered = jax.tree.map(
        lambda a, kind: lax.all_gather(a.astype(kind), axis), shard, (jnp.bfloat16, jnp.bfloat16)
    )
    state = jax.tree.map(lambda a, e: jnp.zeros_like(a) + jnp.asarray(e, a.dtype), shard, neutral)

    def carried_one(step, state):
        source = count - 1 - step
        return join(
            state,
            jax.tree.map(
                lambda a, own: lax.dynamic_index_in_dim(a, source, 0, False).astype(own.dtype),
                gathered,
                shard,
            ),
        )

    return lax.fori_loop(0, ahead, carried_one, state)


def doc_geometry(doc_lengths, positions):
    doc_ends = jnp.cumsum(doc_lengths, axis=1)
    begins = doc_ends - doc_lengths
    doc_ids = jnp.sum((positions[None, :, None] >= doc_ends[:, None, :]).astype(jnp.int32), axis=2)
    starts = jnp.sum((positions[None, :, None] == begins[:, None, :]).astype(jnp.float32), axis=2)
    return (doc_ids, starts)


def chain_join(earlier, later):
    keep = (1.0 - later[1]).reshape((-1,) + (1,) * (later[0].ndim - 1))
    state_sum = later[0] + keep * earlier[0]
    return (state_sum, jnp.maximum(earlier[1], later[1]))


def split_product(form, data, state):
    high_part = state.astype(jnp.bfloat16)
    low_part = (state - lax.optimization_barrier(high_part).astype(jnp.float32)).astype(
        jnp.bfloat16
    )
    first = jnp.einsum(form, data, high_part, preferred_element_type=jnp.float32)
    return first + jnp.einsum(form, data, low_part, preferred_element_type=jnp.float32)


def blocks_math(
    queries, keys, values, grad_output, gain_heads, doc_ids, starts, forward_carry, backward_carry
):
    counted = jnp.cumsum(starts, axis=1)
    totals = counted[:, -1:]
    before = (counted == 0).astype(jnp.float32)[:, :, None, None]
    after_mask = (totals - counted == 0).astype(jnp.float32)[:, :, None, None]
    opened = jnp.minimum(totals[:, 0], 1.0)
    row_ids = jnp.arange(queries.shape[1])
    causal = row_ids[:, None] >= row_ids[None, :]
    doc_mask = jnp.logical_and(causal[None], doc_ids[:, :, None] == doc_ids[:, None, :]).astype(
        jnp.float32
    )[:, None]
    scores = jnp.einsum("btge,bsge->bgts", queries, keys, preferred_element_type=jnp.float32)
    weights = (scores * doc_mask).astype(jnp.bfloat16)
    own_state = jnp.einsum(
        "bsge,bsgf->bgef",
        keys * after_mask.astype(jnp.bfloat16),
        values,
        preferred_element_type=jnp.float32,
    )
    carried = forward_carry(own_state, opened)
    attended = jnp.einsum("bgts,bsgf->btgf", weights, values, preferred_element_type=jnp.float32)
    attended = attended + before * split_product("btge,bgef->btgf", queries, carried)
    root_mean = jnp.sqrt(jnp.mean(attended * attended, axis=-1, keepdims=True) + eps)
    normed = attended / root_mean
    output = (gain_heads * normed).astype(jnp.bfloat16)
    dyf = grad_output.astype(jnp.float32)
    dnormed = dyf * gain_heads
    grad_att = (
        (dnormed - normed * jnp.mean(dnormed * normed, axis=-1, keepdims=True)) / root_mean
    ).astype(jnp.bfloat16)
    gain_part = jnp.sum(dyf * normed, axis=(0, 1))
    grad_scores = jnp.einsum(
        "btgf,bsgf->bgts", grad_att, values, preferred_element_type=jnp.float32
    )
    grad_weights = (grad_scores * doc_mask).astype(jnp.bfloat16)
    back_state = jnp.einsum(
        "btge,btgf->bgef",
        queries * before.astype(jnp.bfloat16),
        grad_att,
        preferred_element_type=jnp.float32,
    )
    back_carried = backward_carry(back_state, opened)
    grad_q = jnp.einsum("bgts,bsge->btge", grad_weights, keys, preferred_element_type=jnp.float32)
    grad_q = grad_q + before * split_product("btgf,bgef->btge", grad_att, carried)
    grad_k = jnp.einsum(
        "bgts,btge->bsge", grad_weights, queries, preferred_element_type=jnp.float32
    )
    grad_k = grad_k + after_mask * split_product("bsgf,bgef->bsge", values, back_carried)
    grad_v = jnp.einsum("bgts,btgf->bsgf", weights, grad_att, preferred_element_type=jnp.float32)
    grad_v = grad_v + after_mask * split_product("bsge,bgef->bsgf", keys, back_carried)
    return (
        output,
        grad_q.astype(jnp.bfloat16),
        grad_k.astype(jnp.bfloat16),
        grad_v.astype(jnp.bfloat16),
        gain_part,
    )


def per_device(queries, keys, values, grad_output, out_gain, doc_lengths):
    local_seqs, block_len, width = queries.shape
    ctx_count = lax.axis_size("ctx")
    ctx_index = lax.axis_index("ctx")
    shape4 = (local_seqs, block_len, H, E)
    quad = tuple((item.reshape(shape4) for item in (queries, keys, values, grad_output)))
    gain_heads = out_gain.reshape(H, E)
    positions = ctx_index * block_len + jnp.arange(block_len, dtype=jnp.int32)
    doc_ids, starts = doc_geometry(doc_lengths, positions)

    def chain_forward(state, opened):
        wide = state.reshape(state.shape[0], H, E * E)
        moved = entering(
            (wide, opened), "ctx", chain_join, (jnp.zeros_like(wide), jnp.zeros_like(opened))
        )[0]
        return moved.reshape(state.shape)

    def chain_backward(state, opened):
        wide = state.reshape(state.shape[0], H, E * E)
        moved = carried_in(
            (wide, opened), "ctx", chain_join, (jnp.zeros_like(wide), jnp.zeros_like(opened))
        )[0]
        return moved.reshape(state.shape)

    results = blocks_math(
        quad[0],
        quad[1],
        quad[2],
        quad[3],
        gain_heads,
        doc_ids,
        starts,
        chain_forward,
        chain_backward,
    )
    returned = results[:4]
    gain_terms = results[4]
    total_tokens = local_seqs * lax.axis_size("dp") * block_len * ctx_count
    grad_gain = lax.psum(gain_terms.reshape(H * E), ("dp", "ctx")) / math.sqrt(total_tokens)
    flat = (local_seqs, block_len, H * E)
    outputs = tuple((item.reshape(flat) for item in returned))
    return (outputs[0], outputs[1], outputs[2], outputs[3], grad_gain)


def solution(mesh):
    placed = (
        P("dp", "ctx", None),
        P("dp", "ctx", None),
        P("dp", "ctx", None),
        P("dp", "ctx", None),
        P(),
        P("dp", None),
    )
    return jax.shard_map(
        per_device,
        mesh=mesh,
        in_specs=placed,
        out_specs=(
            P("dp", "ctx", None),
            P("dp", "ctx", None),
            P("dp", "ctx", None),
            P("dp", "ctx", None),
            P(),
        ),
        check_vma=False,
    )
```

profile of v0, /device:TPU:32, one launch (start us, length us, event | category | flops | bytes accessed | tf_op | source)
XLA Modules:
  0.0 422.3 jit_solution(17803829553141644253)
XLA Ops:
  7.2 0.8 reduce_window_sum.22
  8.1 0.7 subtract_bitcast_fusion
  10.4 1.3 copy.66
  11.7 1.3 copy.67
  13.5 1.2 all_gather_reshape.3
  15.3 1.3 copy.65
  16.7 1.2 copy.70
  18.6 0.7 bitcast_dynamic-update-slice_fusion
  19.2 68.4 %all-reduce = f32[32]{0:T(128)S(1)} all-reduce(f32[32]{0:T(128)S(1)} %bitcast_dynamic-update-slice_fusion), channel_id=1, replica_groups=mesh['dp'=8,'ctx'=32] {'ctx'}, use_global_device_ids=true, to_apply=%add | all-reduce | flops 32 | bytes 256
  88.3 7.0 %all-gather.3.cloned.1.call-done = f32[32,1,32,4096]{3,2,1,0:T(8,128)} async-done(((f32[1,1,32,4096]{3,2,1,0:T(8,128)}), f32[32,1,32,4096]{3,2,1,0:T(8,128)}) %all-gather.3.cloned.1.call-update) | async-done | bytes 16777232 | tf_op jit(solution)/shard_map/all_gather | solution.py:14
  95.4 1.5 reshape.498
  97.8 0.9 copy-done
  99.5 0.8 multiply_reduce_fusion.2
  100.7 0.8 multiply_reduce_fusion
  101.6 1.3 divide_convert_fusion
  103.2 1.2 convert_element_type.251
  104.5 0.8 dynamic-update-slice.1
  105.2 143.0 %all-reduce.1 = bf16[32]{0:T(256)(128)(2,1)S(1)} all-reduce(bf16[32]{0:T(256)(128)(2,1)S(1)} %dynamic-update-slice.1), channel_id=1, replica_groups=mesh['dp'=8,'ctx'=32] {'ctx'}, use_global_device_ids=true, to_apply=%add.1 | all-reduce | flops 32 | bytes 128
  249.9 0.8 copy-done.4
  250.7 0.8 fusion.13
  251.5 1.0 copy.76
  252.5 1.0 copy.75
  253.6 73.1 %psum.7 = f32[2048]{0:T(1024)S(1)} all-reduce(f32[2048]{0:T(1024)S(1)} %reshape.507), channel_id=1, replica_groups=mesh['dp'=8,'ctx'=32] {'dp','ctx'}, use_global_device_ids=true, to_apply=%region_11.12 | all-reduce | flops 2048 | bytes 16384 | tf_op jit(solution)/shard_map/psum | solution.py:170
  327.3 74.7 %while.27 = (s32[]{:T(128)}, f32[1,32,4096]{2,1,0:T(8,128)S(1)}, s32[]{:T(128)}, bf16[32,1,32,4096]{3,2,1,0:T(8,128)(2,1)}, bf16[32,1]{0,1:T(2,128)(2,1)S(1)}, /*index=5*/s32[]{:T(128)}, s32[]{:T(128)}, s32[]{:T(128)}, s32[]{:T(128)}) while((s32[]{:T(128)}, f32[1,32,4096]{2,1,0:T(8,128)S(1)}, s32[]{:T(128)}, ...), condition=%wide.region_9.10_spmd, body=%wide.region_8.9_spmd.sunk | while | flops 393223 | bytes 1310877 | solution.py:45
  328.0 1.8 convert_add_fusion.2
  330.4 1.8 convert_add_fusion.2
  332.8 1.8 convert_add_fusion.2
  335.2 1.8 convert_add_fusion.2
  337.6 1.8 convert_add_fusion.2
  340.0 1.8 convert_add_fusion.2
  342.4 1.8 convert_add_fusion.2
  344.8 1.8 convert_add_fusion.2
  347.2 1.8 convert_add_fusion.2
  349.6 1.8 convert_add_fusion.2
  352.0 1.8 convert_add_fusion.2
  354.4 1.8 convert_add_fusion.2
  356.8 1.8 convert_add_fusion.2
  359.2 1.8 convert_add_fusion.2
  361.6 1.8 convert_add_fusion.2
  364.0 1.8 convert_add_fusion.2
  366.4 1.8 convert_add_fusion.2
  368.8 1.8 convert_add_fusion.2
  371.2 1.8 convert_add_fusion.2
  373.6 1.8 convert_add_fusion.2
  376.0 1.8 convert_add_fusion.2
  378.4 1.8 convert_add_fusion.2
  380.8 1.8 convert_add_fusion.2
  383.2 1.8 convert_add_fusion.2
  385.6 1.8 convert_add_fusion.2
  388.0 1.8 convert_add_fusion.2
  390.4 1.8 convert_add_fusion.2
  392.8 1.8 convert_add_fusion.2
  395.2 1.8 convert_add_fusion.2
  397.6 1.8 convert_add_fusion.2
  400.0 1.8 convert_add_fusion.2
  402.0 1.4 reshape.503
  404.0 1.3 fusion.46
  405.3 1.3 fusion.45
  406.6 1.6 copy.72
  408.3 1.3 copy-done.10
  409.9 0.9 copy-done.3
  411.2 1.0 copy.78
  412.2 1.8 fusion.11
  414.5 1.0 copy.77
  (97 shorter events, 28.5 us)
Async XLA Ops:
  7.2 88.1 %all-gather.3.cloned.1.call-start = ((), (), s32[]{:S(2)}) async-start(), calls=%async_computation | async-start | bytes 17301504 | tf_op jit(solution)/shard_map/all_gather | solution.py:14
  13.4 3.2 copy-start.12
  13.4 4.5 %copy-start.13 = (f32[2048]{0:T(1024)S(1)}, f32[2048]{0:T(1024)}, u32[]{:S(2)}) copy-start(f32[2048]{0:T(1024)} %param.14) | copy-start | bytes 24580
  13.4 4.5 %copy-start.14 = (u32[256]{0:T(256)S(1)}, u32[256]{0:T(256)}, u32[]{:S(2)}) copy-start(u32[256]{0:T(256)} %constant.98) | copy-start | bytes 3076
  14.6 312.7 %all-gather.5.cloned.1.call-start = ((), (), s32[]{:S(2)}) async-start(), calls=%async_computation.1 | async-start | bytes 8650752 | tf_op jit(solution)/shard_map/all_gather | solution.py:30
  88.3 10.8 %copy-start.2 = (bf16[32,128,128]{2,1,0:T(8,128)(2,1)}, bf16[32,128,128]{2,1,0:T(8,128)(2,1)S(1)}, u32[]{:S(2)}) copy-start(bf16[32,128,128]{2,1,0:T(8,128)(2,1)S(1)} %multiply_convert_fusion.1) | copy-start | bytes 3145732
  97.4 1.2 copy-start
  98.7 0.8 copy-start.7
  99.5 1.2 copy-start.6
  248.3 1.2 copy-start.1
  248.3 1.4 copy-start.8
  249.6 1.1 copy-start.4
  250.7 1.8 copy-start.11
  408.1 1.4 copy-start.10
  408.2 1.7 copy-start.9
  409.6 1.2 copy-start.3
  412.2 1.8 copy-start.5
Sparse Core Ops, SparseCore 0:
  14.8 80.4 all-gather.2
  104.6 133.7 all-gather.4
where the time goes:
time: 425 us; the launch traced here: 422 us
  blocking collectives  284 us (67%)
  other arithmetic  79.3 us (19%)
  local copies, waits for them, and re-layouts  25.1 us (6%)
  between operations  15.1 us (4%)
  matrix products  10.3 us (2%)
  waiting for transfers between devices  7.01 us (2%)
    unnamed x2, blocking collectives  211 us
    psum x1, blocking collectives, per_device(): lax.psum(gain_terms.reshape(H * E), ('dp', 'ctx')) / math.sqrt(total_tokens)  73.1 us
    add x31, other arithmetic, chain_join(): state_sum = later[0] + keep * earlier[0]  55.5 us
    sub x31, other arithmetic, chain_join(): keep = (1.0 - later[1]).reshape((-1,) + (1,) * (later[0].ndim - 1))  18.2 us
    unnamed x42, local copies, waits for them, and re-layouts  15.2 us
  transfers between devices with their start and end apart: 2, of which 1 were waited for; matrix products, arithmetic and copies ran while one was open for 2% of the time, Pallas kernels for 0%

commit v1 on v0

--- a/solution.py
+++ b/solution.py
@@ -167,7 +167,9 @@
     returned = results[:4]
     gain_terms = results[4]
     total_tokens = local_seqs * lax.axis_size("dp") * block_len * ctx_count
-    grad_gain = lax.psum(gain_terms.reshape(H * E), ("dp", "ctx")) / math.sqrt(total_tokens)
+    grad_gain = jnp.sum(
+        lax.all_gather(gain_terms.reshape(H * E), ("dp", "ctx")), axis=0
+    ) / math.sqrt(total_tokens)
     flat = (local_seqs, block_len, H * E)
     outputs = tuple((item.reshape(flat) for item in returned))
     return (outputs[0], outputs[1], outputs[2], outputs[3], grad_gain)

time: 425 us -> 440 us (1.035)
  waiting for transfers between devices: 7.01 us -> 90.4 us
  blocking collectives: 284 us -> 211 us
    psum x1 -> x0, blocking collectives: 73.1 us -> none  [per_device(): lax.psum(gain_terms.reshape(H * E), ('dp', 'ctx')) / math.sqrt(total_tokens)]
    all_gather x1, waiting for transfers between devices: 0.01 us -> 56.4 us  [carried_in(): lax.all_gather(a.astype(kind), axis)]
    all_gather x0 -> x1, waiting for transfers between devices: none -> 27 us  [per_device(): lax.all_gather(gain_terms.reshape(H * E), ('dp', 'ctx'))]
    unnamed x42 -> x51, local copies, waits for them, and re-layouts: 15.2 us -> 16.9 us
  transfers between devices with their start and end apart: 2 -> 3, of which waited for: 1 -> 3; matrix products, arithmetic and copies ran while one was open for 2% -> 4% of each run, Pallas kernels for 0% -> 0%
where the time goes in v1:
time: 440 us; the launch traced here: 438 us
  blocking collectives  211 us (48%)
  waiting for transfers between devices  90.4 us (21%)
  other arithmetic  83.3 us (19%)
  local copies, waits for them, and re-layouts  26.7 us (6%)
  between operations  14.8 us (3%)
  matrix products  10.3 us (2%)
    unnamed x2, blocking collectives  211 us
    all_gather x1, waiting for transfers between devices, carried_in(): lax.all_gather(a.astype(kind), axis)  56.4 us
    add x31, other arithmetic, chain_join(): state_sum = later[0] + keep * earlier[0]  55.5 us
    all_gather x1, waiting for transfers between devices, per_device(): lax.all_gather(gain_terms.reshape(H * E), ('dp', 'ctx'))  27 us
    sub x31, other arithmetic, chain_join(): keep = (1.0 - later[1]).reshape((-1,) + (1,) * (later[0].ndim - 1))  18.2 us
    unnamed x51, local copies, waits for them, and re-layouts  16.9 us
  transfers between devices with their start and end apart: 3, of which 3 were waited for; matrix products, arithmetic and copies ran while one was open for 4% of the time, Pallas kernels for 0%

profile of v1, /device:TPU:32, one launch (start us, length us, event | category | flops | bytes accessed | tf_op | source)
XLA Modules:
  0.0 437.5 jit_solution(5215919654126572247)
XLA Ops:
  7.2 0.8 reduce_window_sum.22
  10.4 1.3 copy.66
  11.7 1.3 copy.67
  13.5 1.2 all_gather_reshape.6
  15.3 1.3 copy.65
  16.7 1.2 copy.70
  19.2 68.4 %all-reduce = f32[32]{0:T(128)S(1)} all-reduce(f32[32]{0:T(128)S(1)} %bitcast_dynamic-update-slice_fusion), channel_id=1, replica_groups=mesh['dp'=8,'ctx'=32] {'ctx'}, use_global_device_ids=true, to_apply=%add | all-reduce | flops 32 | bytes 256
  88.3 7.0 %all-gather.5.cloned.1.call-done = f32[32,1,32,4096]{3,2,1,0:T(8,128)} async-done(((f32[1,1,32,4096]{3,2,1,0:T(8,128)}), f32[32,1,32,4096]{3,2,1,0:T(8,128)}) %all-gather.5.cloned.1.call-update) | async-done | bytes 16777232 | tf_op jit(solution)/shard_map/all_gather | solution.py:14
  95.4 1.4 reshape.495
  97.7 1.1 copy-done
  98.8 0.8 copy-done.9
  100.0 0.8 multiply_reduce_fusion.2
  100.9 0.9 copy-done.6
  101.8 0.8 multiply_reduce_fusion
  103.4 2.5 divide_convert_fusion
  106.3 1.2 convert_element_type.251
  108.3 142.5 %all-reduce.1 = bf16[32]{0:T(256)(128)(2,1)S(1)} all-reduce(bf16[32]{0:T(256)(128)(2,1)S(1)} %dynamic-update-slice.1), channel_id=1, replica_groups=mesh['dp'=8,'ctx'=32] {'ctx'}, use_global_device_ids=true, to_apply=%add.1 | all-reduce | flops 32 | bytes 128
  253.1 0.8 fusion.13
  253.9 1.0 copy.76
  255.0 1.0 copy.75
  256.0 27.0 %all-gather.9.cloned.1.call-done = f32[256,1,2048]{2,1,0:T(1,128)} async-done(((f32[1,1,2048]{2,1,0:T(1,128)}), f32[256,1,2048]{2,1,0:T(1,128)}) %all-gather.9.cloned.1.call-update) | async-done | bytes 2097168 | tf_op jit(solution)/shard_map/all_gather | solution.py:171
  283.0 2.8 reduce_sum.62
  286.4 56.4 %all-gather.7.cloned.1.call-done = bf16[32,1,32,4096]{3,2,1,0:T(8,128)(2,1)} async-done(((bf16[1,1,32,4096]{3,2,1,0:T(8,128)(2,1)}), bf16[32,1,32,4096]{3,2,1,0:T(8,128)(2,1)}) %all-gather.7.cloned.1.call-update) | async-done | bytes 8388624 | tf_op jit(solution)/shard_map/all_gather | solution.py:30
  342.8 74.7 %while.27 = (s32[]{:T(128)}, f32[1,32,4096]{2,1,0:T(8,128)S(1)}, s32[]{:T(128)}, bf16[32,1,32,4096]{3,2,1,0:T(8,128)(2,1)}, bf16[32,1]{0,1:T(2,128)(2,1)S(1)}, /*index=5*/s32[]{:T(128)}, s32[]{:T(128)}, s32[]{:T(128)}, s32[]{:T(128)}) while((s32[]{:T(128)}, f32[1,32,4096]{2,1,0:T(8,128)S(1)}, s32[]{:T(128)}, ...), condition=%wide.region_9.10_spmd, body=%wide.region_8.9_spmd.sunk | while | flops 393223 | bytes 1310877 | solution.py:45
  343.4 1.8 convert_add_fusion.2
  345.8 1.8 convert_add_fusion.2
  348.2 1.8 convert_add_fusion.2
  350.6 1.8 convert_add_fusion.2
  353.0 1.8 convert_add_fusion.2
  355.4 1.8 convert_add_fusion.2
  357.8 1.8 convert_add_fusion.2
  360.2 1.8 convert_add_fusion.2
  362.6 1.8 convert_add_fusion.2
  365.0 1.8 convert_add_fusion.2
  367.4 1.8 convert_add_fusion.2
  369.9 1.8 convert_add_fusion.2
  372.3 1.8 convert_add_fusion.2
  374.7 1.8 convert_add_fusion.2
  377.1 1.8 convert_add_fusion.2
  379.5 1.8 convert_add_fusion.2
  381.9 1.8 convert_add_fusion.2
  384.3 1.8 convert_add_fusion.2
  386.7 1.8 convert_add_fusion.2
  389.1 1.8 convert_add_fusion.2
  391.5 1.8 convert_add_fusion.2
  393.9 1.8 convert_add_fusion.2
  396.3 1.8 convert_add_fusion.2
  398.7 1.8 convert_add_fusion.2
  401.1 1.8 convert_add_fusion.2
  403.5 1.8 convert_add_fusion.2
  405.9 1.8 convert_add_fusion.2
  408.3 1.8 convert_add_fusion.2
  410.7 1.8 convert_add_fusion.2
  413.1 1.8 convert_add_fusion.2
  415.5 1.8 convert_add_fusion.2
  417.5 1.5 reshape.500
  419.5 1.3 fusion.46
  420.8 1.3 fusion.45
  422.1 1.6 copy.72
  423.8 1.3 copy-done.14
  425.4 0.9 copy-done.3
  426.7 1.0 copy.78
  427.7 1.8 fusion.11
  430.0 1.0 copy.77
  (108 shorter events, 31.1 us)
Async XLA Ops:
  7.2 88.1 %all-gather.5.cloned.1.call-start = ((), (), s32[]{:S(2)}) async-start(), calls=%async_computation | async-start | bytes 17301504 | tf_op jit(solution)/shard_map/all_gather | solution.py:14
  13.4 3.2 copy-start.16
  13.4 4.5 %copy-start.17 = (f32[2048]{0:T(1024)S(1)}, f32[2048]{0:T(1024)}, u32[]{:S(2)}) copy-start(f32[2048]{0:T(1024)} %param.14) | copy-start | bytes 24580
  13.4 4.5 %copy-start.18 = (u32[256]{0:T(256)S(1)}, u32[256]{0:T(256)}, u32[]{:S(2)}) copy-start(u32[256]{0:T(256)} %constant.98) | copy-start | bytes 3076
  14.6 268.4 %all-gather.9.cloned.1.call-start = ((), (), s32[]{:S(2)}) async-start(), calls=%async_computation.2 | async-start | bytes 2105344 | tf_op jit(solution)/shard_map/all_gather | solution.py:171
  88.3 11.7 %copy-start.2 = (bf16[32,128,128]{2,1,0:T(8,128)(2,1)}, bf16[32,128,128]{2,1,0:T(8,128)(2,1)S(1)}, u32[]{:S(2)}) copy-start(bf16[32,128,128]{2,1,0:T(8,128)(2,1)S(1)} %multiply_convert_fusion.1) | copy-start | bytes 3145732
  97.3 2.7 copy-start.12
  97.3 1.4 copy-start
  98.8 0.8 copy-start.9
  100.0 1.8 copy-start.7
  100.9 1.0 copy-start.6
  100.9 2.6 copy-start.8
  103.4 239.4 %all-gather.7.cloned.1.call-start = ((), (), s32[]{:S(2)}) async-start(), calls=%async_computation.1 | async-start | bytes 8650752 | tf_op jit(solution)/shard_map/all_gather | solution.py:30
  105.9 144.9 %copy-start.13 = (bf16[32,64,64]{2,1,0:T(8,128)(2,1)S(1)}, bf16[32,64,64]{2,1,0:T(8,128)(2,1)}, u32[]{:S(2)}) copy-start(bf16[32,64,64]{2,1,0:T(8,128)(2,1)} %copy-done.12) | copy-start | bytes 786436
  250.8 1.2 copy-start.1
  250.8 1.4 copy-start.10
  252.1 1.0 copy-start.4
  253.1 1.8 copy-start.15
  423.7 1.4 copy-start.14
  423.8 1.7 copy-start.11
  425.1 1.2 copy-start.3
  427.7 1.8 copy-start.5
Sparse Core Ops, SparseCore 0:
  14.7 80.4 all-gather.4
  103.5 179.4 all-gather.8
  285.6 57.1 all-gather.6
